TPU v7x, 32 devices: a whole 2x2x4 slice. The times are simulated.
32 devices in a mesh: seq: 8 (over z, x), stream: 4 (over y, core).
Axes of the slice: x: 2, y: 2, z: 4, core: 2. Of those that a mesh axis runs over, the one named last changes fastest.
Arguments:
- tokens: bfloat16 [4, 4096, 768], P('stream', 'seq'), may hold values from -6 to 6
- segment_ids: int32 [4, 4096], P('stream', 'seq'), may hold values from -1 to 32, as said below
- query_key_value_weight: bfloat16 [768, 2304], replicated, may hold values from -0.21875 to 0.21875
- conv_kernel: bfloat16 [3, 2304], replicated, may hold values from -3 to 3
- attention_output_weight: bfloat16 [768, 768], replicated, may hold values from -0.875 to 0.875
- up_weight: bfloat16 [768, 3072], replicated, may hold values from -0.21875 to 0.21875
- down_weight: bfloat16 [3072, 768], replicated, may hold values from -0.109375 to 0.109375
- gain_attn: bfloat16 [768], replicated, may hold values from 0.5 to 1.5
- shift_attn: bfloat16 [768], replicated, may hold values from -3 to 3
- gain_ffn: bfloat16 [768], replicated, may hold values from 0.5 to 1.5
- shift_ffn: bfloat16 [768], replicated, may hold values from -3 to 3
- cotangent: bfloat16 [4, 4096, 768], P('stream', 'seq'), may hold values from -6 to 6
Outputs:
- out_tokens: bfloat16 [4, 4096, 768], P('stream', 'seq')
- grad_tokens: float32 [4, 4096, 768], P('stream', 'seq')
- grad_w_qkv: float32 [768, 2304], replicated
- grad_conv_kernel: float32 [3, 2304], replicated
- grad_w_out: float32 [768, 768], replicated
- grad_w_up: float32 [768, 3072], replicated
- grad_w_down: float32 [3072, 768], replicated
- grad_gain_attn: float32 [768], replicated
- grad_shift_attn: float32 [768], replicated
- grad_gain_ffn: float32 [768], replicated
- grad_shift_ffn: float32 [768], replicated
Inputs may be any that keep to these rules, and one draw needn't show every extreme that they name: `segment_ids`: along each pack the document numbers never fall and differ between documents; each document fills 128 to 256 consecutive slots, one of 256 slots in every pack; the last document of every pack has the number 4096 // 128; slots between documents hold -1, and so does the last slot of each pack.
All inputs are finite; a program needn't handle non-finite values.
Results may differ from a plain program's by a relative error of at most 0.019.
Values may be sent and summed in bfloat16 or wider, within the bound.
No kernel may reach another device: no remote copies, remote signals or barrier semaphores. Data moves between devices by JAX's collectives and lax.ppermute only.
A program may use at most 256 MiB of HBM per device.

v0:
```python
import math
import jax
import jax.numpy as jnp
from jax import lax
from jax.sharding import PartitionSpec as P

H = 12
HD = 64
EPSILON = 1e-05
MASKED = -1e30


def passed_along(block, axis, distance):
    devices = range(lax.axis_size(axis))
    route = [(i - distance, i) for i in devices if i - distance in devices]
    return lax.ppermute(block, axis, route)


def layer_norm(field, gain, shift):
    center = field - jnp.mean(field, -1, keepdims=True)
    spread = jnp.mean(center * center, -1, keepdims=True)
    return center * lax.rsqrt(spread + EPSILON) * gain + shift


def square_relu(field):
    return jnp.square(jnp.maximum(field, 0.0))


def conv_local(extended, kernel, same_one, same_two):
    row_count = extended.shape[1] - 2
    result = kernel[0] * extended[:, 2:]
    result = result + kernel[1] * extended[:, 1 : row_count + 1] * same_one
    result = result + kernel[2] * extended[:, :row_count] * same_two
    return result


def pair_scores(queries, key_rows, query_ids, key_ids, query_pos, key_pos):
    raw_scores = jnp.einsum(
        "sqhd,skhd->shqk", queries, key_rows, preferred_element_type=jnp.float32
    )
    allowed = (query_ids[:, :, None] == key_ids[:, None, :]) & (key_ids[:, None, :] >= 0)
    allowed = (
        allowed
        & (key_pos[None, None, :] <= query_pos[None, :, None])
        & (key_pos[None, None, :] >= 0)
    )
    allowed = allowed | (key_pos[None, None, :] == query_pos[None, :, None])
    return jnp.where(allowed[:, None], raw_scores * (1.0 / math.sqrt(HD)), MASKED)


def on_device(
    tokens,
    segment_ids,
    query_key_value_weight,
    conv_kernel,
    attention_output_weight,
    up_weight,
    down_weight,
    gain_attn,
    shift_attn,
    gain_ffn,
    shift_ffn,
    cotangent,
):
    pack_count, slot_count, model_width = tokens.shape
    device_at = lax.axis_index("seq")
    slot_steps = jnp.arange(slot_count, dtype=jnp.int32)
    query_pos = device_at * slot_count + slot_steps
    own_live = segment_ids >= 0
    active_token_mask = own_live.astype(jnp.float32)[..., None]
    inputs = tokens.astype(jnp.float32)
    normalized_first, norm_one_back = jax.vjp(
        layer_norm, inputs, gain_attn.astype(jnp.float32), shift_attn.astype(jnp.float32)
    )
    normalized_first_narrow = normalized_first.astype(jnp.bfloat16)
    mixed_query_key_value = jnp.einsum(
        "jmc,ct->jmt",
        normalized_first_narrow,
        query_key_value_weight,
        preferred_element_type=jnp.float32,
    )
    halo_rows, halo_ids = passed_along(
        (mixed_query_key_value[:, -2:], segment_ids[:, -2:]), "seq", 1
    )
    extended = jnp.concatenate([halo_rows, mixed_query_key_value], 1)
    extended_ids = jnp.concatenate([halo_ids, segment_ids], 1)
    same_one = ((extended_ids[:, 1 : slot_count + 1] == segment_ids) & own_live).astype(
        jnp.float32
    )[..., None]
    same_two = ((extended_ids[:, :slot_count] == segment_ids) & own_live).astype(jnp.float32)[
        ..., None
    ]
    convolved, conv_back = jax.vjp(
        lambda field, weights: conv_local(field, weights, same_one, same_two),
        extended,
        conv_kernel.astype(jnp.float32),
    )
    conv_low = convolved.astype(jnp.bfloat16)
    head_shape = (pack_count, slot_count, H, HD)
    queries = conv_low[..., :model_width].reshape(head_shape)
    pair_kv = conv_low[..., model_width:]
    prior_kv, prior_ids = passed_along((pair_kv, segment_ids), "seq", 1)
    shard_kv = jnp.stack([prior_kv, pair_kv])
    shard_ids = jnp.stack([prior_ids, segment_ids])
    shard_at = device_at - 1 + jnp.arange(2, dtype=jnp.int32)
    shard_total = shard_kv.shape[0]
    first_id = jnp.min(jnp.where(own_live, segment_ids, 1 << 30))

    def shard_view(shard):
        block_kv = lax.dynamic_index_in_dim(shard_kv, shard, 0, keepdims=False)
        key_rows = block_kv[..., :model_width].reshape(head_shape)
        value_rows = block_kv[..., model_width:].reshape(head_shape)
        key_ids = lax.dynamic_index_in_dim(shard_ids, shard, 0, keepdims=False)
        owner = lax.dynamic_index_in_dim(shard_at, shard, 0, keepdims=False)
        key_pos = owner * slot_count + slot_steps
        useful = (owner == device_at) | (owner < device_at) & (owner >= 0) & (
            jnp.max(key_ids) >= first_id
        )
        return (key_rows, value_rows, key_ids, key_pos, useful)

    def keep_state(state):
        return state

    def top_step(shard, state):
        key_rows, value_rows, key_ids, key_pos, useful = shard_view(shard)

        def top_work(inner):
            row_top, row_total = inner
            scores = pair_scores(queries, key_rows, segment_ids, key_ids, query_pos, key_pos)
            new_top = jnp.maximum(row_top, jnp.max(scores, -1))
            row_total = row_total * jnp.exp(row_top - new_top) + jnp.sum(
                jnp.exp(scores - new_top[..., None]), -1
            )
            return (new_top, row_total)

        return lax.cond(useful, top_work, keep_state, state)

    stat_shape = (pack_count, H, slot_count)
    row_top, row_total = lax.fori_loop(
        0,
        shard_total,
        top_step,
        (jnp.full(stat_shape, MASKED, jnp.float32), jnp.zeros(stat_shape, jnp.float32)),
    )
    log_total = row_top + jnp.log(row_total)

    def probs_for(key_rows, key_ids, key_pos):
        scores = pair_scores(queries, key_rows, segment_ids, key_ids, query_pos, key_pos)
        return jnp.exp(scores - log_total[..., None])

    def out_step(shard, state):
        key_rows, value_rows, key_ids, key_pos, useful = shard_view(shard)

        def out_work(inner):
            probs = probs_for(key_rows, key_ids, key_pos)
            return inner + jnp.einsum(
                "shqk,skhd->sqhd",
                probs.astype(jnp.bfloat16),
                value_rows,
                preferred_element_type=jnp.float32,
            )

        return lax.cond(useful, out_work, keep_state, state)

    attention_result = lax.fori_loop(0, shard_total, out_step, jnp.zeros(head_shape, jnp.float32))
    attention_result = attention_result.reshape(pack_count, slot_count, model_width).astype(
        jnp.bfloat16
    )
    residual_branch = jnp.einsum(
        "jmc,ct->jmt", attention_result, attention_output_weight, preferred_element_type=jnp.float32
    )
    middle_state = inputs + active_token_mask * residual_branch
    normalized_second, norm_two_back = jax.vjp(
        layer_norm, middle_state, gain_ffn.astype(jnp.float32), shift_ffn.astype(jnp.float32)
    )
    normalized_second_narrow = normalized_second.astype(jnp.bfloat16)
    hidden_state = jnp.einsum(
        "zha,ay->zhy", normalized_second_narrow, up_weight, preferred_element_type=jnp.float32
    )
    activated_hidden, relu_back = jax.vjp(square_relu, hidden_state)
    activated_narrow = activated_hidden.astype(jnp.bfloat16)
    feedforward_output = jnp.einsum(
        "nxg,gi->nxi", activated_narrow, down_weight, preferred_element_type=jnp.float32
    )
    out_tokens = (middle_state + active_token_mask * feedforward_output).astype(jnp.bfloat16)
    grad_out = cotangent.astype(jnp.float32)
    gradient_residual_branch = (active_token_mask * grad_out).astype(jnp.bfloat16)
    grad_w_down = jnp.einsum(
        "ipr,iph->rh",
        activated_narrow,
        gradient_residual_branch,
        preferred_element_type=jnp.float32,
    )
    gradient_activated = jnp.einsum(
        "owr,ar->owa", gradient_residual_branch, down_weight, preferred_element_type=jnp.float32
    )
    gradient_hidden_state = relu_back(gradient_activated)[0].astype(jnp.bfloat16)
    grad_w_up = jnp.einsum(
        "jtw,jth->wh",
        normalized_second_narrow,
        gradient_hidden_state,
        preferred_element_type=jnp.float32,
    )
    grad_normed_two = jnp.einsum(
        "ytw,pw->ytp", gradient_hidden_state, up_weight, preferred_element_type=jnp.float32
    )
    grad_middle_part, grad_gain_ffn, grad_shift_ffn = norm_two_back(grad_normed_two)
    grad_middle = grad_out + grad_middle_part
    gradient_attention_branch = (active_token_mask * grad_middle).astype(jnp.bfloat16)
    grad_w_out = jnp.einsum(
        "tir,tiv->rv",
        attention_result,
        gradient_attention_branch,
        preferred_element_type=jnp.float32,
    )
    grad_heads = (
        jnp.einsum(
            "tig,ag->tia",
            gradient_attention_branch,
            attention_output_weight,
            preferred_element_type=jnp.float32,
        )
        .astype(jnp.bfloat16)
        .reshape(head_shape)
    )

    def delta_step(shard, state):
        key_rows, value_rows, key_ids, key_pos, useful = shard_view(shard)

        def delta_work(inner):
            probs = probs_for(key_rows, key_ids, key_pos)
            grad_probs = jnp.einsum(
                "sqhd,skhd->shqk", grad_heads, value_rows, preferred_element_type=jnp.float32
            )
            return inner + jnp.sum(probs * grad_probs, -1)

        return lax.cond(useful, delta_work, keep_state, state)

    row_delta = lax.fori_loop(0, shard_total, delta_step, jnp.zeros(stat_shape, jnp.float32))

    def grad_step(shard, state):
        key_rows, value_rows, key_ids, key_pos, useful = shard_view(shard)

        def grad_work(inner):
            grad_queries, key_terms = inner
            probs = probs_for(key_rows, key_ids, key_pos)
            grad_probs = jnp.einsum(
                "sqhd,skhd->shqk", grad_heads, value_rows, preferred_element_type=jnp.float32
            )
            grad_scores = (
                probs * (grad_probs - row_delta[..., None]) * (1.0 / math.sqrt(HD))
            ).astype(jnp.bfloat16)
            grad_queries = grad_queries + jnp.einsum(
                "shqk,skhd->sqhd", grad_scores, key_rows, preferred_element_type=jnp.float32
            )
            grad_keys = jnp.einsum(
                "shqk,sqhd->skhd", grad_scores, queries, preferred_element_type=jnp.float32
            )
            grad_values = jnp.einsum(
                "shqk,sqhd->skhd",
                probs.astype(jnp.bfloat16),
                grad_heads,
                preferred_element_type=jnp.float32,
            )
            key_piece = jnp.concatenate(
                [
                    grad_keys.reshape(pack_count, slot_count, model_width),
                    grad_values.reshape(pack_count, slot_count, model_width),
                ],
                -1,
            )
            key_terms = lax.dynamic_update_index_in_dim(key_terms, key_piece, shard, 0)
            return (grad_queries, key_terms)

        return lax.cond(useful, grad_work, keep_state, state)

    term_init = jnp.zeros((shard_total, pack_count, slot_count, 2 * model_width), jnp.float32)
    grad_queries, key_terms = lax.fori_loop(
        0, shard_total, grad_step, (jnp.zeros(head_shape, jnp.float32), term_init)
    )
    grad_kv = key_terms[1] + passed_along(key_terms[0].astype(jnp.bfloat16), "seq", -1).astype(
        jnp.float32
    )
    grad_conv = jnp.concatenate(
        [grad_queries.reshape(pack_count, slot_count, model_width), grad_kv], -1
    )
    grad_extended, grad_kernel = conv_back(grad_conv)
    back_rows = passed_along(grad_extended[:, :2], "seq", -1)
    gradient_mixed_projection = grad_extended[:, 2:]
    gradient_mixed_projection = jnp.concatenate(
        [gradient_mixed_projection[:, :-2], gradient_mixed_projection[:, -2:] + back_rows], 1
    ).astype(jnp.bfloat16)
    grad_w_qkv = jnp.einsum(
        "tir,tiv->rv",
        normalized_first_narrow,
        gradient_mixed_projection,
        preferred_element_type=jnp.float32,
    )
    gradient_normalized_first = jnp.einsum(
        "tig,ag->tia",
        gradient_mixed_projection,
        query_key_value_weight,
        preferred_element_type=jnp.float32,
    )
    grad_input_part, grad_gain_attn, grad_shift_attn = norm_one_back(gradient_normalized_first)
    grad_tokens = grad_middle + grad_input_part
    grads = [
        grad_w_qkv,
        grad_kernel,
        grad_w_out,
        grad_w_up,
        grad_w_down,
        grad_gain_attn,
        grad_shift_attn,
        grad_gain_ffn,
        grad_shift_ffn,
    ]
    flat = jnp.concatenate([piece.reshape(-1) for piece in grads])
    shares = lax.psum_scatter(
        flat.astype(jnp.bfloat16), "seq", scatter_dimension=0, tiled=True
    ).astype(jnp.float32)
    shares = lax.psum(shares.astype(jnp.bfloat16), "stream").astype(jnp.float32)
    summed = lax.all_gather(shares.astype(jnp.bfloat16), "seq", axis=0, tiled=True).astype(
        shares.dtype
    )
    results = []
    offset = 0
    for piece in grads:
        count = piece.size
        results.append(summed[offset : offset + count].reshape(piece.shape))
        offset = offset + count
    return (
        out_tokens,
        grad_tokens,
        results[0],
        results[1],
        results[2],
        results[3],
        results[4],
        results[5],
        results[6],
        results[7],
        results[8],
    )


def solution(mesh):
    return jax.shard_map(
        on_device,
        mesh=mesh,
        in_specs=(
            P("stream", "seq", None),
            P("stream", "seq"),
            P(),
            P(),
            P(),
            P(),
            P(),
            P(),
            P(),
            P(),
            P(),
            P("stream", "seq", None),
        ),
        out_specs=(
            P("stream", "seq", None),
            P("stream", "seq", None),
            P(),
            P(),
            P(),
            P(),
            P(),
            P(),
            P(),
            P(),
            P(),
        ),
        check_vma=False,
    )
```

profile of v0, /device:TPU:0, one launch (start us, length us, event | category | flops | bytes accessed | tf_op | source)
XLA Modules:
  0.0 1588.4 jit_solution(7274010136364462006)
XLA Ops:
  41.8 25.5 %collective-permute-done = s32[1,512]{1,0:T(1,128)S(1)} collective-permute-done((s32[1,512]{1,0:T(1,128)S(1)}, s32[1,512]{1,0:T(1,128)S(1)}, u32[]{:S(2)}, u32[]{:S(2)}) %collective-permute-start) | collective-permute-done | bytes 2080 | tf_op jit(solution)/shard_map/ppermute | solution.py:16
  81.4 21.0 %while.66 = (s32[]{:T(128)}, f32[1,12,512]{2,1,0:T(8,128)}, f32[1,12,512]{2,1,0:T(8,128)}, s32[2]{0:T(128)}, s32[]{:T(128)}, /*index=5*/s32[2,1,512]{2,1,0:T(1,1...) while((s32[]{:T(128)}, f32[1,12,512]{2,1,0:T(8,128)}, ...), condition=%wide.region_9.10_spmd.clone, body=%wide.region_3.9_spmd.clone.sunk | while | flops 426523136 | bytes 36882872 | solution.py:139
  91.6 10.8 conditional.12
  105.1 23.4 %while.67 = (s32[]{:T(128)}, f32[1,512,12,64]{1,3,2,0:T(8,128)}, s32[2]{0:T(128)}, s32[]{:T(128)}, s32[2,1,512]{2,1,0:T(1,128)S(1)}, /*index=5*/s32[]{:T(128)}, ...) while((s32[]{:T(128)}, f32[1,512,12,64]{1,3,2,0:T(8,128)}, ...), condition=%wide.region_14.15_spmd.clone, body=%wide.region_10.14_spmd.clone.sunk | while | flops 820120064 | bytes 12372291 | solution.py:165
  115.8 12.2 conditional.13
  150.8 21.0 %while.68 = (s32[]{:T(128)}, f32[1,12,512]{2,1,0:T(8,128)}, s32[2]{0:T(128)}, s32[]{:T(128)}, s32[2,1,512]{2,1,0:T(1,128)S(1)}, /*index=5*/s32[]{:T(128)}, s32[1...) while((s32[]{:T(128)}, f32[1,12,512]{2,1,0:T(8,128)}, ...), condition=%wide.region_24.25_spmd.clone, body=%wide.region_19.24_spmd.clone.sunk | while | flops 822872576 | bytes 41666984 | solution.py:239
  161.2 10.5 conditional.14
  176.6 41.2 %while.69 = (s32[]{:T(128)}, f32[1,512,12,64]{1,3,2,0:T(8,128)}, f32[2,1,512,1536]{2,3,1,0:T(8,128)}, s32[2]{0:T(128)}, s32[]{:T(128)}, /*index=5*/s32[2,1,512]{...) while((s32[]{:T(128)}, f32[1,512,12,64]{1,3,2,0:T(8,128)}, ...), condition=%wide.region_29.30_spmd.clone, body=%wide.region_25.29_spmd.clone.sunk | while | flops 2050886144 | bytes 144902832 | solution.py:278
  187.7 30.1 %conditional.15 = ((f32[1,512,12,64]{1,3,2,0:T(8,128)}, f32[2,1,512,1536]{2,3,1,0:T(8,128)})) conditional(s32[]{:T(128)} %convert_element_type.256, (f32[1,512,12,64]{1,3,2,0:T(8,128)}, f32[2,1,512,1536]{2,3,1,0:T(8,128)}) %tuple.244, (bf16[2,1,512,1536]{2,3,1,0:T(8,128)(2,1)}, s32[]{:T(128)}, s32[1,512]{1,0:T(1,128)S(1)}, ...), branch_computations={%region_27.27_spmd, %region_28.28_spmd} | conditional | flops 2050885632 | bytes 144896320 | solution.py:275
  228.9 7.9 convolution_convert_fusion
  236.7 9.4 reshape.1646
  268.4 59.5 %collective-permute-done.4 = bf16[1,512,1536]{2,1,0:T(8,128)(2,1)} collective-permute-done((bf16[1,512,1536]{2,1,0:T(8,128)(2,1)}, bf16[1,512,1536]{2,1,0:T(8,128)(2,1)}, u32[]{:S(2)}, u32[]{:S(2)}) %collective-permute-start.4) | collective-permute-done | bytes 1572896 | tf_op jit(solution)/shard_map/ppermute | solution.py:16
  388.7 19.2 %dynamic-update-slice.3 = bf16[7087872]{0:T(1024)(128)(2,1)} dynamic-update-slice(bf16[7087872]{0:T(1024)(128)(2,1)} %dynamic-update-slice.2, bf16[589824]{0:T(1024)(128)(2,1)} %reshape.1644, s32[]{} %constant.348) | dynamic-update-slice | bytes 2359300
  407.9 72.5 %dynamic-update-slice.4 = bf16[7087872]{0:T(1024)(128)(2,1)} dynamic-update-slice(bf16[7087872]{0:T(1024)(128)(2,1)} %dynamic-update-slice.3, bf16[2359296]{0:T(1024)(128)(2,1)} %bitcast.265, s32[]{} %constant.349) | dynamic-update-slice | bytes 9437188
  480.5 72.4 %dynamic-update-slice.5 = bf16[7087872]{0:T(1024)(128)(2,1)} dynamic-update-slice(bf16[7087872]{0:T(1024)(128)(2,1)} %dynamic-update-slice.4, bf16[2359296]{0:T(1024)(128)(2,1)} %reshape.1646, s32[]{} %constant.350) | dynamic-update-slice | bytes 9437188
  559.5 444.2 %all-reduce.16.cloned.1.call-done = bf16[7087872]{0:T(1024)(128)(2,1)} async-done(((bf16[7087872]{0:T(1024)(128)(2,1)}), bf16[7087872]{0:T(1024)(128)(2,1)}) %all-reduce.16.cloned.1.call-update) | async-done | bytes 14175760
  1008.2 44.8 %all-reduce.12.cloned.1.call-done = bf16[885984]{0:T(1024)(128)(2,1)} async-done(((bf16[885984]{0:T(1024)(128)(2,1)}), bf16[885984]{0:T(1024)(128)(2,1)}) %all-reduce.12.cloned.1.call-update) | async-done | bytes 1771984 | tf_op jit(solution)/shard_map/psum | solution.py:322
  1058.1 28.2 %dynamic-update-slice = bf16[7087872]{0:T(1024)(128)(2,1)} dynamic-update-slice(bf16[7087872]{0:T(1024)(128)(2,1)} %broadcast.947, bf16[885984]{0:T(1024)(128)(2,1)} %all-reduce.12.cloned.1.call-done, u32[]{:T(128)} %bitcast.83) | dynamic-update-slice | bytes 3543940
  1087.0 8.4 fusion.78
  1097.4 428.8 %all-reduce.14.cloned.1.call-done = bf16[7087872]{0:T(1024)(128)(2,1)} async-done(((bf16[7087872]{0:T(1024)(128)(2,1)}), bf16[7087872]{0:T(1024)(128)(2,1)}) %all-reduce.14.cloned.1.call-update) | async-done | bytes 14175760
  1539.9 8.2 reshape.1647
  1548.1 10.0 fusion.112
  1558.1 11.3 slice.198
  1569.4 10.9 reshape.1649
  (362 shorter events, 280.8 us)
Async XLA Ops:
  7.2 996.4 %all-reduce.16.cloned.1.call-start = ((), (), s32[]{:S(2)}) async-start(), calls=%async_computation.2 | async-start | bytes 28352512
  8.1 16.2 %collective-permute-start.2 = (s32[1,2]{1,0:T(1,128)S(1)}, s32[1,2]{1,0:T(1,128)S(1)}, u32[]{:S(2)}, u32[]{:S(2)}) collective-permute-start(s32[1,2]{1,0:T(1,128)S(1)} %slice.180), channel_id=1, source_target_pairs={{0,4},{4,8},{8,12},{12,16},{16,20},{20,24},{24,28},{1,5},{5,9},{9,... | collective-permute-start | bytes 32 | tf_op jit(solution)/shard_map/ppermute | solution.py:16
  20.7 4.9 collective-permute-start.1
  28.1 12.5 copy-start.80
  28.1 13.1 copy-start.81
  30.6 41.1 %collective-permute-start.3 = (bf16[1,512,1536]{2,1,0:T(8,128)(2,1)}, bf16[1,512,1536]{2,1,0:T(8,128)(2,1)}, u32[]{:S(2)}, u32[]{:S(2)}) collective-permute-start(bf16[1,512,1536]{2,1,0:T(8,128)(2,1)} %get-tuple-element.1763), channel_id=1, source_target_pairs={{0,4},{4,8},{8,12},{12,16},{16,20},{20,24},{24,28},{1,5},{5,9},{9,... | collective-permute-start | bytes 4718600 | tf_op jit(solution)/shard_map/ppermute | solution.py:16
  35.9 31.4 %collective-permute-start = (s32[1,512]{1,0:T(1,128)S(1)}, s32[1,512]{1,0:T(1,128)S(1)}, u32[]{:S(2)}, u32[]{:S(2)}) collective-permute-start(s32[1,512]{1,0:T(1,128)S(1)} %copy-done.27), channel_id=1, source_target_pairs={{0,4},{4,8},{8,12},{12,16},{16,20},{20,24},{24,28},{1,5},{5,9},{9,... | collective-permute-start | bytes 6152 | tf_op jit(solution)/shard_map/ppermute | solution.py:16
  227.6 100.3 %collective-permute-start.4 = (bf16[1,512,1536]{2,1,0:T(8,128)(2,1)}, bf16[1,512,1536]{2,1,0:T(8,128)(2,1)}, u32[]{:S(2)}, u32[]{:S(2)}) collective-permute-start(bf16[1,512,1536]{2,1,0:T(8,128)(2,1)} %fusion.75), channel_id=1, source_target_pairs={{4,0},{8,4},{12,8},{16,12},{20,16},{24,20},{28,24},{5,1},{9,5},{13... | collective-permute-start | bytes 4718600 | tf_op jit(solution)/shard_map/ppermute | solution.py:16
  236.7 11.5 copy-start.71
  236.7 11.5 copy-start.79
  268.4 62.3 %copy-start.22 = (f32[1,512,768]{2,1,0:T(8,128)S(1)}, f32[1,512,768]{2,1,0:T(8,128)}, u32[]{:S(2)}) copy-start(f32[1,512,768]{2,1,0:T(8,128)} %copy.68) | copy-start | bytes 4718596
  268.4 62.3 %copy-start.35 = (f32[2304]{0:T(1024)S(1)}, f32[2304]{0:T(1024)}, u32[]{:S(2)}) copy-start(f32[2304]{0:T(1024)} %copy-done.34) | copy-start | bytes 27652
  268.4 62.3 %copy-start.37 = (f32[2304]{0:T(1024)S(1)}, f32[2304]{0:T(1024)}, u32[]{:S(2)}) copy-start(f32[2304]{0:T(1024)} %copy-done.36) | copy-start | bytes 27652
  268.4 62.3 %copy-start.39 = (f32[2304]{0:T(1024)S(1)}, f32[2304]{0:T(1024)}, u32[]{:S(2)}) copy-start(f32[2304]{0:T(1024)} %copy-done.38) | copy-start | bytes 27652
  268.4 62.3 %copy-start.41 = (f32[1,2,2304]{2,1,0:T(2,128)S(1)}, f32[1,2,2304]{2,1,0:T(2,128)}, u32[]{:S(2)}) copy-start(f32[1,2,2304]{2,1,0:T(2,128)} %copy-done.40) | copy-start | bytes 55300
  268.4 62.3 %copy-start.62 = (f32[1,512]{1,0:T(1,128)S(1)}, f32[1,512]{1,0:T(1,128)}, u32[]{:S(2)}) copy-start(f32[1,512]{1,0:T(1,128)} %copy-done.61) | copy-start | bytes 6148
  268.4 62.3 %copy-start.64 = (f32[1,512]{1,0:T(1,128)S(1)}, f32[1,512]{1,0:T(1,128)}, u32[]{:S(2)}) copy-start(f32[1,512]{1,0:T(1,128)} %copy-done.63) | copy-start | bytes 6148
  351.0 11.2 collective-permute-start.5
  480.4 72.4 %copy-start.75 = (bf16[768]{0:T(1024)(128)(2,1)S(1)}, bf16[768]{0:T(1024)(128)(2,1)}, u32[]{:S(2)}) copy-start(bf16[768]{0:T(1024)(128)(2,1)} %get-tuple-element.1627) | copy-start | bytes 4612
  480.4 73.8 %copy-start.74 = (bf16[768]{0:T(1024)(128)(2,1)S(1)}, bf16[768]{0:T(1024)(128)(2,1)}, u32[]{:S(2)}) copy-start(bf16[768]{0:T(1024)(128)(2,1)} %reduce_sum.178) | copy-start | bytes 4612
  480.4 75.2 %copy-start.83 = (bf16[768]{0:T(1024)(128)(2,1)S(1)}, bf16[768]{0:T(1024)(128)(2,1)}, u32[]{:S(2)}) copy-start(bf16[768]{0:T(1024)(128)(2,1)} %get-tuple-element.1625) | copy-start | bytes 4612
  480.4 76.5 %copy-start.72 = (bf16[768]{0:T(1024)(128)(2,1)S(1)}, bf16[768]{0:T(1024)(128)(2,1)}, u32[]{:S(2)}) copy-start(bf16[768]{0:T(1024)(128)(2,1)} %reduce_sum.183) | copy-start | bytes 4612
  557.6 495.4 %all-reduce.12.cloned.1.call-start = ((), (), s32[]{:S(2)}) async-start(), calls=%async_computation | async-start | bytes 3547136 | tf_op jit(solution)/shard_map/psum | solution.py:322
  1007.3 518.9 %all-reduce.14.cloned.1.call-start = ((), (), s32[]{:S(2)}) async-start(), calls=%async_computation.1 | async-start | bytes 28352512
  (79 other events, 387.9 us)
Sparse Core Ops, SparseCore 0:
  557.7 445.8 all-reduce.15
  1007.4 45.4 all-reduce.11
  1086.5 439.7 all-reduce.13
where the time goes:
time: 1620 us; the launch traced here: 1590 us
  waiting for transfers between devices  1010 us (62%)
  local copies, waits for them, and re-layouts  363 us (22%)
  matrix products  86.2 us (5%)
  other arithmetic  62.3 us (4%)
  loops' own time  30.1 us (2%)
  starting transfers between devices  20.5 us (1%)
  between operations  16.3 us (1%)
    unnamed x5, waiting for transfers between devices  873 us
    unnamed x174, local copies, waits for them, and re-layouts  228 us
    ppermute x6, waiting for transfers between devices, passed_along(): return lax.ppermute(block, axis, route)  91.8 us
    psum x1, waiting for transfers between devices, on_device(): shares = lax.psum(shares.astype(jnp.bfloat16), 'stream').astype(jnp.float32)  44.8 us
    slice x7, local copies, waits for them, and re-layouts, on_device(): results.append(summed[offset:offset + count].reshape(piece.shape))  34.9 us
  transfers between devices with their start and end apart: 9, of which 7 were waited for; matrix products, arithmetic and copies ran while one was open for 4% of the time, Pallas kernels for 0%

commit v1 on v0

--- a/solution.py
+++ b/solution.py
@@ -8,6 +8,12 @@
 HD = 64
 EPSILON = 1e-05
 MASKED = -1e30
+
+
+def summed_here(x, mesh_axis):
+    parts = lax.all_gather(x, mesh_axis, axis=0, tiled=False)
+    total = parts.sum(axis=0)
+    return total
 
 
 def passed_along(block, axis, distance):
@@ -319,7 +325,7 @@
     shares = lax.psum_scatter(
         flat.astype(jnp.bfloat16), "seq", scatter_dimension=0, tiled=True
     ).astype(jnp.float32)
-    shares = lax.psum(shares.astype(jnp.bfloat16), "stream").astype(jnp.float32)
+    shares = summed_here(shares.astype(jnp.bfloat16), "stream").astype(jnp.float32)
     summed = lax.all_gather(shares.astype(jnp.bfloat16), "seq", axis=0, tiled=True).astype(
         shares.dtype
     )

time: 1620 us -> 1780 us (1.099)
  waiting for transfers between devices: 1010 us -> 1090 us
  local copies, waits for them, and re-layouts: 363 us -> 405 us
  other arithmetic: 62.3 us -> 99.1 us
    unnamed x5 -> x6, waiting for transfers between devices: 873 us -> 1000 us
    psum x1 -> x0, waiting for transfers between devices: 44.8 us -> none  [on_device(): shares = lax.psum(shares.astype(jnp.bfloat16), 'stream').astype(jnp.float32)]
    reduce_sum x0 -> x1, other arithmetic: none -> 37.1 us  [summed_here(): total = parts.sum(axis=0)]
    unnamed x174 -> x179, local copies, waits for them, and re-layouts: 228 us -> 260 us
where the time goes in v1:
time: 1780 us; the launch traced here: 1750 us
  waiting for transfers between devices  1090 us (61%)
  local copies, waits for them, and re-layouts  405 us (23%)
  other arithmetic  99.1 us (6%)
  matrix products  86.2 us (5%)
  loops' own time  28.3 us (2%)
  starting transfers between devices  20.3 us (1%)
    unnamed x6, waiting for transfers between devices  1000 us
    unnamed x179, local copies, waits for them, and re-layouts  260 us
    ppermute x6, waiting for transfers between devices, passed_along(): return lax.ppermute(block, axis, route)  91.8 us
    reduce_sum x1, other arithmetic, summed_here(): total = parts.sum(axis=0)  37.1 us
  transfers between devices with their start and end apart: 9, of which 7 were waited for; matrix products, arithmetic and copies ran while one was open for 4% of the time, Pallas kernels for 0%

profile of v1, /device:TPU:0, one launch (start us, length us, event | category | flops | bytes accessed | tf_op | source)
XLA Modules:
  0.0 1751.1 jit_solution(10227578031631669933)
XLA Ops:
  41.8 25.4 %collective-permute-done = s32[1,512]{1,0:T(1,128)S(1)} collective-permute-done((s32[1,512]{1,0:T(1,128)S(1)}, s32[1,512]{1,0:T(1,128)S(1)}, u32[]{:S(2)}, u32[]{:S(2)}) %collective-permute-start) | collective-permute-done | bytes 2080 | tf_op jit(solution)/shard_map/ppermute | solution.py:22
  81.4 20.8 %while.66 = (s32[]{:T(128)}, f32[1,12,512]{2,1,0:T(8,128)}, f32[1,12,512]{2,1,0:T(8,128)}, s32[2]{0:T(128)}, s32[]{:T(128)}, /*index=5*/s32[2,1,512]{2,1,0:T(1,1...) while((s32[]{:T(128)}, f32[1,12,512]{2,1,0:T(8,128)}, ...), condition=%wide.region_9.10_spmd.clone, body=%wide.region_3.9_spmd.clone.sunk | while | flops 426523136 | bytes 36882872 | solution.py:145
  91.4 10.8 conditional.12
  104.9 22.3 %while.67 = (s32[]{:T(128)}, f32[1,512,12,64]{1,3,2,0:T(8,128)}, s32[2]{0:T(128)}, s32[]{:T(128)}, s32[2,1,512]{2,1,0:T(1,128)S(1)}, /*index=5*/s32[]{:T(128)}, ...) while((s32[]{:T(128)}, f32[1,512,12,64]{1,3,2,0:T(8,128)}, ...), condition=%wide.region_14.15_spmd.clone, body=%wide.region_10.14_spmd.clone.sunk | while | flops 820120064 | bytes 12372291 | solution.py:171
  115.0 12.2 conditional.13
  149.5 20.5 %while.68 = (s32[]{:T(128)}, f32[1,12,512]{2,1,0:T(8,128)}, s32[2]{0:T(128)}, s32[]{:T(128)}, s32[2,1,512]{2,1,0:T(1,128)S(1)}, /*index=5*/s32[]{:T(128)}, s32[1...) while((s32[]{:T(128)}, f32[1,12,512]{2,1,0:T(8,128)}, ...), condition=%wide.region_24.25_spmd.clone, body=%wide.region_19.24_spmd.clone.sunk | while | flops 822872576 | bytes 41666984 | solution.py:245
  159.5 10.5 conditional.14
  174.9 40.2 %while.69 = (s32[]{:T(128)}, f32[1,512,12,64]{1,3,2,0:T(8,128)}, f32[2,1,512,1536]{2,3,1,0:T(8,128)}, s32[2]{0:T(128)}, s32[]{:T(128)}, /*index=5*/s32[2,1,512]{...) while((s32[]{:T(128)}, f32[1,512,12,64]{1,3,2,0:T(8,128)}, ...), condition=%wide.region_29.30_spmd.clone, body=%wide.region_25.29_spmd.clone.sunk | while | flops 2050886144 | bytes 144902832 | solution.py:284
  185.0 30.0 %conditional.15 = ((f32[1,512,12,64]{1,3,2,0:T(8,128)}, f32[2,1,512,1536]{2,3,1,0:T(8,128)})) conditional(s32[]{:T(128)} %convert_element_type.258, (f32[1,512,12,64]{1,3,2,0:T(8,128)}, f32[2,1,512,1536]{2,3,1,0:T(8,128)}) %tuple.248, (bf16[2,1,512,1536]{2,3,1,0:T(8,128)(2,1)}, s32[]{:T(128)}, s32[1,512]{1,0:T(1,128)S(1)}, ...), branch_computations={%region_27.27_spmd, %region_28.28_spmd} | conditional | flops 2050885632 | bytes 144896320 | solution.py:281
  234.0 9.6 reshape.1646
  265.9 59.0 %collective-permute-done.4 = bf16[1,512,1536]{2,1,0:T(8,128)(2,1)} collective-permute-done((bf16[1,512,1536]{2,1,0:T(8,128)(2,1)}, bf16[1,512,1536]{2,1,0:T(8,128)(2,1)}, u32[]{:S(2)}, u32[]{:S(2)}) %collective-permute-start.4) | collective-permute-done | bytes 1572896 | tf_op jit(solution)/shard_map/ppermute | solution.py:22
  386.0 19.2 %dynamic-update-slice.4 = bf16[7087872]{0:T(1024)(128)(2,1)} dynamic-update-slice(bf16[7087872]{0:T(1024)(128)(2,1)} %dynamic-update-slice.3, bf16[589824]{0:T(1024)(128)(2,1)} %reshape.1644, s32[]{} %constant.356) | dynamic-update-slice | bytes 2359300
  405.2 72.4 %dynamic-update-slice.5 = bf16[7087872]{0:T(1024)(128)(2,1)} dynamic-update-slice(bf16[7087872]{0:T(1024)(128)(2,1)} %dynamic-update-slice.4, bf16[2359296]{0:T(1024)(128)(2,1)} %bitcast.266, s32[]{} %constant.357) | dynamic-update-slice | bytes 9437188
  477.7 72.4 %dynamic-update-slice.6 = bf16[7087872]{0:T(1024)(128)(2,1)} dynamic-update-slice(bf16[7087872]{0:T(1024)(128)(2,1)} %dynamic-update-slice.5, bf16[2359296]{0:T(1024)(128)(2,1)} %reshape.1646, s32[]{} %constant.358) | dynamic-update-slice | bytes 9437188
  557.9 442.7 %all-reduce.17.cloned.1.call-done = bf16[7087872]{0:T(1024)(128)(2,1)} async-done(((bf16[7087872]{0:T(1024)(128)(2,1)}), bf16[7087872]{0:T(1024)(128)(2,1)}) %all-reduce.17.cloned.1.call-update) | async-done | bytes 14175760
  1007.5 28.3 %dynamic-update-slice = bf16[3543936]{0:T(1024)(128)(2,1)} dynamic-update-slice(bf16[3543936]{0:T(1024)(128)(2,1)} %broadcast.947, bf16[885984]{0:T(1024)(128)(2,1)} %dynamic-slice.3, u32[]{:T(128)} %bitcast.83) | dynamic-update-slice | bytes 3543940
  1036.4 131.3 %all-reduce.13.cloned.1.call-done = bf16[3543936]{0:T(1024)(128)(2,1)} async-done(((bf16[3543936]{0:T(1024)(128)(2,1)}), bf16[3543936]{0:T(1024)(128)(2,1)}) %all-reduce.13.cloned.1.call-update) | async-done | bytes 7087888
  1167.8 10.7 reshape.1653
  1178.5 37.1 %reduce_sum.198 = bf16[885984]{0:T(1024)(128)(2,1)} reduce(bf16[4,885984]{1,0:T(4,128)(2,1)} %reshape.1653, bf16[]{:T(256)} %constant.314.clone.1), dimensions={0}, to_apply=%region_40.41 | reduce | flops 2657952 | bytes 8859842 | tf_op jit(solution)/shard_map/reduce_sum | solution.py:15
  1220.7 28.2 %dynamic-update-slice.1 = bf16[7087872]{0:T(1024)(128)(2,1)} dynamic-update-slice(bf16[7087872]{0:T(1024)(128)(2,1)} %broadcast.948, bf16[885984]{0:T(1024)(128)(2,1)} %reduce_sum.198, u32[]{:T(128)} %bitcast.84) | dynamic-update-slice | bytes 3543940
  1260.0 428.9 %all-reduce.15.cloned.1.call-done = bf16[7087872]{0:T(1024)(128)(2,1)} async-done(((bf16[7087872]{0:T(1024)(128)(2,1)}), bf16[7087872]{0:T(1024)(128)(2,1)}) %all-reduce.15.cloned.1.call-update) | async-done | bytes 14175760
  1710.7 10.1 fusion.112
  1720.8 11.3 slice.198
  1732.1 10.9 reshape.1649
  (369 shorter events, 308.3 us)
Async XLA Ops:
  7.2 993.4 %all-reduce.17.cloned.1.call-start = ((), (), s32[]{:S(2)}) async-start(), calls=%async_computation.2 | async-start | bytes 28352512
  8.1 16.2 collective-permute-start.2
  20.7 4.9 collective-permute-start.1
  28.1 12.5 copy-start.80
  28.1 13.1 copy-start.81
  30.6 41.1 %collective-permute-start.3 = (bf16[1,512,1536]{2,1,0:T(8,128)(2,1)}, bf16[1,512,1536]{2,1,0:T(8,128)(2,1)}, u32[]{:S(2)}, u32[]{:S(2)}) collective-permute-start(bf16[1,512,1536]{2,1,0:T(8,128)(2,1)} %get-tuple-element.1811), channel_id=1, source_target_pairs={{0,4},{4,8},{8,12},{12,16},{16,20},{20,24},{24,28},{1,5},{5,9},{9,... | collective-permute-start | bytes 4718600 | tf_op jit(solution)/shard_map/ppermute | solution.py:22
  35.9 31.4 %collective-permute-start = (s32[1,512]{1,0:T(1,128)S(1)}, s32[1,512]{1,0:T(1,128)S(1)}, u32[]{:S(2)}, u32[]{:S(2)}) collective-permute-start(s32[1,512]{1,0:T(1,128)S(1)} %copy-done.27), channel_id=1, source_target_pairs={{0,4},{4,8},{8,12},{12,16},{16,20},{20,24},{24,28},{1,5},{5,9},{9,... | collective-permute-start | bytes 6152 | tf_op jit(solution)/shard_map/ppermute | solution.py:22
  224.8 100.1 %collective-permute-start.4 = (bf16[1,512,1536]{2,1,0:T(8,128)(2,1)}, bf16[1,512,1536]{2,1,0:T(8,128)(2,1)}, u32[]{:S(2)}, u32[]{:S(2)}) collective-permute-start(bf16[1,512,1536]{2,1,0:T(8,128)(2,1)} %fusion.75), channel_id=1, source_target_pairs={{4,0},{8,4},{12,8},{16,12},{20,16},{24,20},{28,24},{5,1},{9,5},{13... | collective-permute-start | bytes 4718600 | tf_op jit(solution)/shard_map/ppermute | solution.py:22
  234.0 11.7 copy-start.71
  234.0 11.7 copy-start.79
  265.9 61.9 %copy-start.22 = (f32[1,512,768]{2,1,0:T(8,128)S(1)}, f32[1,512,768]{2,1,0:T(8,128)}, u32[]{:S(2)}) copy-start(f32[1,512,768]{2,1,0:T(8,128)} %copy.83) | copy-start | bytes 4718596
  265.9 61.9 %copy-start.35 = (f32[2304]{0:T(1024)S(1)}, f32[2304]{0:T(1024)}, u32[]{:S(2)}) copy-start(f32[2304]{0:T(1024)} %copy-done.34) | copy-start | bytes 27652
  265.9 61.9 %copy-start.37 = (f32[2304]{0:T(1024)S(1)}, f32[2304]{0:T(1024)}, u32[]{:S(2)}) copy-start(f32[2304]{0:T(1024)} %copy-done.36) | copy-start | bytes 27652
  265.9 61.9 %copy-start.39 = (f32[2304]{0:T(1024)S(1)}, f32[2304]{0:T(1024)}, u32[]{:S(2)}) copy-start(f32[2304]{0:T(1024)} %copy-done.38) | copy-start | bytes 27652
  265.9 61.9 %copy-start.41 = (f32[1,2,2304]{2,1,0:T(2,128)S(1)}, f32[1,2,2304]{2,1,0:T(2,128)}, u32[]{:S(2)}) copy-start(f32[1,2,2304]{2,1,0:T(2,128)} %copy-done.40) | copy-start | bytes 55300
  265.9 61.9 %copy-start.62 = (f32[1,512]{1,0:T(1,128)S(1)}, f32[1,512]{1,0:T(1,128)}, u32[]{:S(2)}) copy-start(f32[1,512]{1,0:T(1,128)} %copy-done.61) | copy-start | bytes 6148
  265.9 61.9 %copy-start.64 = (f32[1,512]{1,0:T(1,128)S(1)}, f32[1,512]{1,0:T(1,128)}, u32[]{:S(2)}) copy-start(f32[1,512]{1,0:T(1,128)} %copy-done.63) | copy-start | bytes 6148
  348.0 11.4 collective-permute-start.5
  477.7 72.4 %copy-start.75 = (bf16[768]{0:T(1024)(128)(2,1)S(1)}, bf16[768]{0:T(1024)(128)(2,1)}, u32[]{:S(2)}) copy-start(bf16[768]{0:T(1024)(128)(2,1)} %get-tuple-element.1675) | copy-start | bytes 4612
  477.7 73.8 %copy-start.74 = (bf16[768]{0:T(1024)(128)(2,1)S(1)}, bf16[768]{0:T(1024)(128)(2,1)}, u32[]{:S(2)}) copy-start(bf16[768]{0:T(1024)(128)(2,1)} %reduce_sum.192) | copy-start | bytes 4612
  477.7 75.1 %copy-start.83 = (bf16[768]{0:T(1024)(128)(2,1)S(1)}, bf16[768]{0:T(1024)(128)(2,1)}, u32[]{:S(2)}) copy-start(bf16[768]{0:T(1024)(128)(2,1)} %get-tuple-element.1673) | copy-start | bytes 4612
  477.7 76.5 %copy-start.73 = (bf16[768]{0:T(1024)(128)(2,1)S(1)}, bf16[768]{0:T(1024)(128)(2,1)}, u32[]{:S(2)}) copy-start(bf16[768]{0:T(1024)(128)(2,1)} %reduce_sum.197) | copy-start | bytes 4612
  554.8 613.0 %all-reduce.13.cloned.1.call-start = ((), (), s32[]{:S(2)}) async-start(), calls=%async_computation | async-start | bytes 14176256
  1035.7 653.2 %all-reduce.15.cloned.1.call-start = ((), (), s32[]{:S(2)}) async-start(), calls=%async_computation.1 | async-start | bytes 28352512
  (80 other events, 391.3 us)
Sparse Core Ops, SparseCore 0:
  554.9 445.6 all-reduce.16
  1035.9 131.8 all-reduce.12
  1249.1 439.7 all-reduce.14
